TPU v7x, 128 devices: a whole 4x4x4 slice. The times are simulated.
128 devices in a mesh: ta: 8 (over z, core), af: 16 (over x, y).
Axes of the slice: x: 4, y: 4, z: 4, core: 2. Of those that a mesh axis runs over, the one named last changes fastest.
Arguments:
- velocity: float32 [16, 512, 128, 128], P(None, ('ta', 'af')), may hold values from -14 to 14
- initial_basis: float32 [512, 64], replicated, may hold values from -6 to 6
Outputs:
- core: float32 [16, 128, 64, 128], P('ta', 'af')
All inputs are finite; a program needn't handle non-finite values.
Results may differ from a plain program's by a relative error of at most 0.00017.
Values sent between devices are 32-bit elements; how exact they have to be, the bound alone decides.
A program may use at most 64 MiB of HBM per device.

v0:
```python
import jax
import jax.numpy as jnp
from jax import lax
from jax.sharding import PartitionSpec as P

ITERS = 3


def orthonormal(product):
    lower = jnp.linalg.cholesky(
        jnp.dot(
            product.T, product, precision=lax.Precision.HIGHEST, preferred_element_type=jnp.float32
        )
    )
    return jax.scipy.linalg.solve_triangular(lower, product.T, lower=True).T


def local(velocity, initial_basis):
    groups_ta = lax.axis_size("ta")
    groups_af = lax.axis_size("af")
    frames, slab_planes, cells_x, cells_y = velocity.shape
    planes_total = initial_basis.shape[0]
    blocked = velocity.reshape(
        groups_ta, frames // groups_ta, slab_planes, groups_af, cells_x // groups_af, cells_y
    )
    blocked = blocked.transpose(0, 3, 1, 2, 4, 5).reshape(
        groups_ta * groups_af, frames // groups_ta, slab_planes, cells_x // groups_af, cells_y
    )
    fibres = lax.all_to_all(blocked, ("ta", "af"), split_axis=0, concat_axis=2, tiled=True)
    fibres = fibres.reshape(frames // groups_ta, planes_total, cells_x // groups_af, cells_y)
    gram_local = jnp.einsum(
        "fzxy,fwxy->zw",
        fibres,
        fibres,
        precision=lax.Precision.HIGHEST,
        preferred_element_type=jnp.float32,
    )
    gram_matrix = lax.psum(gram_local, ("ta", "af"))
    subspace = initial_basis
    for iteration in range(ITERS):
        subspace = orthonormal(
            jnp.dot(
                gram_matrix,
                subspace,
                precision=lax.Precision.HIGHEST,
                preferred_element_type=jnp.float32,
            )
        )
    return jnp.einsum(
        "fzxy,zk->fxky",
        fibres,
        subspace,
        precision=lax.Precision.HIGHEST,
        preferred_element_type=jnp.float32,
    )


def solution(mesh):
    placed = (P(None, ("ta", "af"), None, None), P())
    return jax.shard_map(
        local, mesh=mesh, in_specs=placed, out_specs=P("ta", "af", None, None), check_vma=False
    )
```

profile of v0, /device:TPU:1, one launch (start us, length us, event | category | flops | bytes accessed | tf_op | source)
XLA Modules:
  0.0 287.6 jit_solution(15660621444785246462)
XLA Ops:
  6.5 0.0 copy-start
  6.5 0.0 all-reduce.2.cloned.1.call-start
  6.5 5.0 %copy.7 = f32[8,2,4,16,8,128]{5,2,4,1,3,0:T(4,128)S(1)} copy(f32[8,2,4,16,8,128]{5,4,3,2,1,0:T(8,128)} %bitcast.74) | data formatting | bytes 8388608 | tf_op jit(solution)/shard_map/reshape | solution.py:23
  11.5 64.0 %all_to_all.15 = f32[128,2,4,8,128]{4,2,3,1,0:T(4,128)S(1)} all-to-all(f32[128,2,4,8,128]{4,2,3,1,0:T(4,128)S(1)} %bitcast.73), channel_id=1, replica_groups=mesh['ta'=8,'af'=16] {'ta','af'}, dimensions={0} | all-to-all | bytes 8388608 | tf_op jit(solution)/shard_map/all_to_all | solution.py:29
  75.5 1.0 copy.8
  76.5 0.0 copy-start.1
  76.5 1.9 copy-done.1
  78.4 7.9 %convolution_bitcast_fusion = f32[512,512]{1,0:T(8,128)} fusion(f32[2,512,8,128]{3,1,2,0:T(8,128)S(1)} %bitcast.70), kind=kOutput, calls=%fused_computation | convolution fusion | flops 6442450944 | bytes 5242880 | tf_op jit(solution)/shard_map/fzxy,fwxy->zw/dot_general | solution.py:31
  86.3 0.0 all-reduce.2.cloned.1.call-update
  86.3 144.4 %all-reduce.2.cloned.1.call-done = f32[512,512]{1,0:T(8,128)} async-done(((f32[512,512]{1,0:T(8,128)}), f32[512,512]{1,0:T(8,128)}) %all-reduce.2.cloned.1.call-update) | async-done | bytes 1048592 | tf_op jit(solution)/shard_map/psum | solution.py:38
  230.7 0.0 copy-done
  230.7 0.0 copy-start.2
  230.7 2.4 fusion.18
  233.2 0.3 fusion.19
  233.4 0.1 copy.9
  233.5 5.8 %cholesky.59 = f32[64,64]{1,0:T(8,128)S(1)} custom-call(f32[64,64]{1,0:T(8,128)S(1)} %fusion.13), custom_call_target="Cholesky" | custom-call | tf_op jit(solution)/shard_map/jit(cholesky)/cholesky | solution.py:10
  239.4 0.6 compare_reduce_fusion.2
  240.1 0.7 fusion.5
  240.7 4.9 %custom-call.7 = f32[1,64,64]{1,2,0:T(8,128)S(1)} custom-call(f32[1,64,64]{2,1,0:T(8,128)S(1)} %fusion.5), custom_call_target="InvertDiagBlocksLowerTriangular" | custom-call | tf_op jit(solution)/shard_map/jit(_solve_triangular)/triangular_solve | solution.py:15
  245.6 0.3 fusion.3
  246.0 2.4 fusion.20
  248.3 0.3 fusion.21
  248.6 0.1 copy.10
  248.7 6.0 %cholesky.70 = f32[64,64]{1,0:T(8,128)S(1)} custom-call(f32[64,64]{1,0:T(8,128)S(1)} %fusion.11), custom_call_target="Cholesky" | custom-call | tf_op jit(solution)/shard_map/jit(cholesky)/cholesky | solution.py:10
  254.7 0.6 compare_reduce_fusion.1
  255.4 0.7 fusion.6
  256.0 4.9 %custom-call.8 = f32[1,64,64]{1,2,0:T(8,128)S(1)} custom-call(f32[1,64,64]{2,1,0:T(8,128)S(1)} %fusion.6), custom_call_target="InvertDiagBlocksLowerTriangular" | custom-call | tf_op jit(solution)/shard_map/jit(_solve_triangular)/triangular_solve | solution.py:15
  260.9 0.3 fusion.1
  261.3 0.0 copy-done.2
  261.3 1.1 fusion.22
  262.4 0.3 fusion.23
  262.7 0.1 copy.11
  262.8 5.8 %cholesky.81 = f32[64,64]{1,0:T(8,128)S(1)} custom-call(f32[64,64]{1,0:T(8,128)S(1)} %fusion.9), custom_call_target="Cholesky" | custom-call | tf_op jit(solution)/shard_map/jit(cholesky)/cholesky | solution.py:10
  268.6 0.6 compare_reduce_fusion
  269.3 0.7 fusion.7
  269.9 4.9 %custom-call.9 = f32[1,64,64]{1,2,0:T(8,128)S(1)} custom-call(f32[1,64,64]{2,1,0:T(8,128)S(1)} %fusion.7), custom_call_target="InvertDiagBlocksLowerTriangular" | custom-call | tf_op jit(solution)/shard_map/jit(_solve_triangular)/triangular_solve | solution.py:15
  274.8 0.3 convolution_bitcast_fusion.2
  275.2 5.6 %convolution_bitcast_fusion.1 = f32[2,8,64,128]{3,2,1,0:T(8,128)} fusion(f32[64,512,1,1]{1,0,3,2:T(8,128)S(1)} %convolution_bitcast_fusion.2, f32[2,512,8,128]{3,1,2,0:T(8,128)} %bitcast.71), kind=kOutput, calls=%fused_computation.1 | convolution fusion | flops 805306368 | bytes 4849664 | tf_op jit(solution)/shard_map/fzxy,zk->fxky/dot_general | solution.py:49
  (6 shorter events, 0.1 us)
Async XLA Ops:
  6.5 224.2 %copy-start = (f32[512,64]{0,1:T(8,128)S(1)}, f32[512,64]{0,1:T(8,128)}, u32[]{:S(2)}) copy-start(f32[512,64]{0,1:T(8,128)} %param.6) | copy-start | bytes 393220
  6.5 224.2 %all-reduce.2.cloned.1.call-start = ((), (), s32[]{:S(2)}) async-start(), calls=%async_computation.1 | async-start | bytes 2097152 | tf_op jit(solution)/shard_map/psum | solution.py:38
  76.5 1.9 copy-start.1
  230.7 30.5 %copy-start.2 = (f32[512,512]{1,0:T(8,128)S(1)}, f32[512,512]{1,0:T(8,128)}, u32[]{:S(2)}) copy-start(f32[512,512]{1,0:T(8,128)} %all-reduce.2.cloned.1.call-done) | copy-start | bytes 3145732
Sparse Core Ops, SparseCore 0:
  86.5 144.2 all-reduce.1
where the time goes:
time: 288 us
  waiting for transfers between devices  144 us (50%)
  blocking collectives  64 us (22%)
  other arithmetic  36.4 us (13%)
  matrix products  21.3 us (7%)
  between operations  13.5 us (5%)
  local copies, waits for them, and re-layouts  8.09 us (3%)
    psum x1, waiting for transfers between devices, local(): gram_matrix = lax.psum(gram_local, ('ta', 'af'))  144 us
    all_to_all x1, blocking collectives, local(): lax.all_to_all(blocked, ('ta', 'af'), split_axis=0, concat_axis=2, tiled=...  64 us
    another operation x9, other arithmetic, orthonormal(): jnp.linalg.cholesky(jnp.dot(product.T, product, precision=lax.Precision.H...  19.7 us
    another operation x6, other arithmetic, orthonormal(): return jax.scipy.linalg.solve_triangular(lower, product.T, lower=True).T  16.6 us
    dot_general x1, matrix products, local(): jnp.einsum('fzxy,fwxy->zw', fibres, fibres, precision=lax.Precision.HIGHE...  7.93 us
    dot_general x3, matrix products, local(): jnp.dot(gram_matrix, subspace, precision=lax.Precision.HIGHEST, preferred...  5.94 us
  transfers between devices with their start and end apart: 1, of which 1 were waited for; matrix products, arithmetic and copies ran while one was open for 0% of the time, Pallas kernels for 0%

commit v1 on v0

v1 whole, which is shorter than its diff:
```python
import functools
import itertools
import random

import jax
import jax.numpy as jnp
from jax import lax
from jax.experimental import pallas as pl
from jax.experimental.pallas import tpu as pltpu
from jax.sharding import PartitionSpec as P

ITERS = 3
MESH = pl.DeviceIdType.MESH
HIGHEST = lax.Precision.HIGHEST
F32, BF16 = jnp.float32, jnp.bfloat16
NN = (((1,), (0,)), ((), ()))
NT = (((1,), (1,)), ((), ()))


def offsets(n_ta, n_af):
    order = [o for o in itertools.product(range(n_ta), range(n_af)) if o != (0, 0)]
    random.Random(0).shuffle(order)
    return order


def split(value):
    high = value.astype(BF16)
    return high, (value - high.astype(F32)).astype(BF16)


def dot(a, b, dims):
    return lax.dot_general(a, b, dims, preferred_element_type=F32)


def wait_bytes(ref, sem):
    pltpu.make_async_copy(ref, ref, sem).wait()


def regroup_kernel(
    n_ta, n_af, velocity, gram, high_out, low_out, fibres, high, low, partial, pieces,
    send_sem, recv_sem, own_sem, out_sem, rs_send, rs_recv, ag_send, ag_recv,
):
    n = n_ta * n_af
    ta, af = lax.axis_index("ta"), lax.axis_index("af")
    me = ta * n_af + af
    frames, planes, cells = fibres.shape[0], velocity.shape[1], fibres.shape[2]
    order = offsets(n_ta, n_af)
    tas = [lax.rem(ta + i, n_ta) for i in range(n_ta)]
    afs = [lax.rem(af + i, n_af) for i in range(n_af)]

    own = []
    for f in range(frames):
        copy = pltpu.make_async_copy(
            velocity.at[frames * ta + f, :, pl.ds(cells * af, cells), :],
            fibres.at[f, pl.ds(planes * me, planes)],
            own_sem.at[f],
        )
        copy.start()
        own.append(copy)

    barrier = pltpu.get_barrier_semaphore()
    for i, j in order:
        pl.semaphore_signal(barrier, inc=1, device_id=(tas[i], afs[j]), device_id_type=MESH)
    pl.semaphore_wait(barrier, n - 1)

    for f in range(frames):
        for i, j in order:
            pltpu.make_async_remote_copy(
                src_ref=velocity.at[frames * tas[i] + f, :, pl.ds(cells * afs[j], cells), :],
                dst_ref=fibres.at[f, pl.ds(planes * me, planes)],
                send_sem=send_sem,
                recv_sem=recv_sem.at[f],
                device_id=(tas[i], afs[j]),
                device_id_type=MESH,
            ).start()

    outs = []
    for f in range(frames):
        own[f].wait()
        wait_bytes(fibres.at[f, pl.ds(0, planes * (n - 1))], recv_sem.at[f])
        for x in range(cells):
            h, l = split(fibres[f, :, x, :])
            high[f, :, 128 * x : 128 * x + 128] = h
            low[f, :, 128 * x : 128 * x + 128] = l
        for src, dst, s in ((high, high_out, 0), (low, low_out, 1)):
            copy = pltpu.make_async_copy(src.at[f], dst.at[f], out_sem.at[f, s])
            copy.start()
            outs.append(copy)
        for half in range(2):
            rows = pl.ds(256 * half, 256)
            term = (
                dot(high[f], high[f, rows, :], NT)
                + dot(low[f], high[f, rows, :], NT)
                + dot(high[f], low[f, rows, :], NT)
            )
            partial[half] = term if f == 0 else partial[half] + term
    wait_bytes(fibres.at[:, pl.ds(0, planes * (n - 1))], send_sem)

    rows = partial.shape[1] // (n // 2)
    for i, j in order:
        d = tas[i] * n_af + afs[j]
        pltpu.make_async_remote_copy(
            src_ref=partial.at[d // (n // 2), pl.ds(pl.multiple_of(rows * lax.rem(d, n // 2), rows), rows)],
            dst_ref=pieces.at[me],
            send_sem=rs_send,
            recv_sem=rs_recv,
            device_id=(tas[i], afs[j]),
            device_id_type=MESH,
        ).start()
    mine = (me // (n // 2), pl.ds(pl.multiple_of(rows * lax.rem(me, n // 2), rows), rows))
    pieces[me] = partial[mine]
    wait_bytes(pieces.at[pl.ds(0, n - 1)], rs_recv)
    gram[mine] = jnp.sum(pieces[...], axis=0)
    for i, j in order:
        pltpu.make_async_remote_copy(
            src_ref=gram.at[mine],
            dst_ref=gram.at[mine],
            send_sem=ag_send,
            recv_sem=ag_recv,
            device_id=(tas[i], afs[j]),
            device_id_type=MESH,
        ).start()
    wait_bytes(pieces.at[pl.ds(0, n - 1)], rs_send)
    wait_bytes(pieces.at[pl.ds(0, n - 1)], ag_send)
    wait_bytes(pieces.at[pl.ds(0, n - 1)], ag_recv)
    for copy in outs:
        copy.wait()


def regroup(velocity, n_ta, n_af):
    frames, planes, cells, cells_y = velocity.shape
    n = n_ta * n_af
    f, z, x = frames // n_ta, planes * n, cells // n_af
    return pl.pallas_call(
        functools.partial(regroup_kernel, n_ta, n_af),
        name="regroup",
        out_shape=(
            jax.ShapeDtypeStruct((2, z, z // 2), F32),
            jax.ShapeDtypeStruct((f, z, x * cells_y), BF16),
            jax.ShapeDtypeStruct((f, z, x * cells_y), BF16),
        ),
        in_specs=[pl.BlockSpec(memory_space=pl.ANY)],
        out_specs=(
            pl.BlockSpec(memory_space=pltpu.VMEM),
            pl.BlockSpec(memory_space=pl.ANY),
            pl.BlockSpec(memory_space=pl.ANY),
        ),
        scratch_shapes=[
            pltpu.VMEM((f, z, x, cells_y), F32),
            pltpu.VMEM((f, z, x * cells_y), BF16),
            pltpu.VMEM((f, z, x * cells_y), BF16),
            pltpu.VMEM((2, z, z // 2), F32),
            pltpu.VMEM((n, 2 * z // n, z // 2), F32),
            pltpu.SemaphoreType.DMA,
            pltpu.SemaphoreType.DMA((f,)),
            pltpu.SemaphoreType.DMA((f,)),
            pltpu.SemaphoreType.DMA((f, 2)),
            pltpu.SemaphoreType.DMA,
            pltpu.SemaphoreType.DMA,
            pltpu.SemaphoreType.DMA,
            pltpu.SemaphoreType.DMA,
        ],
        compiler_params=pltpu.CompilerParams(
            collective_id=0, has_side_effects=True, vmem_limit_bytes=48 * 2**20
        ),
    )(velocity)


def inverse_cholesky(matrix):
    k, width = matrix.shape
    groups = k // 8
    rows = [matrix[8 * r : 8 * r + 8, :] for r in range(groups)]
    sublane = lax.broadcasted_iota(jnp.int32, (8, width), 0)
    spread = lambda v, c: jnp.broadcast_to(v[c : c + 1, :], (8, width))
    pivots = []
    for g in range(groups):
        columns = [
            [jnp.broadcast_to(rows[r][:, 8 * g + c : 8 * g + c + 1], (8, width)) for r in range(g, groups)]
            for c in range(8)
        ]
        diagonal = None
        for c in range(8):
            pivot = spread(columns[c][0], c)
            diagonal = pivot if c == 0 else jnp.where(sublane == c, pivot, diagonal)
            inverse = pl.reciprocal(pivot, approx=False)
            pivot_row = spread(rows[g], c)
            pivot_columns = {d: spread(columns[d][0], c) for d in range(c + 1, 8)}
            for r in range(g, groups):
                factor = columns[c][r - g] * inverse
                if r == g:
                    factor = jnp.where(sublane > c, factor, 0.0)
                rows[r] = rows[r] - factor * pivot_row
                for d in range(c + 1, 8):
                    columns[d][r - g] = columns[d][r - g] - factor * pivot_columns[d]
        pivots.append(diagonal)
    scaled = []
    for r in range(groups):
        root = lax.rsqrt(pivots[r])
        root = root * (1.5 - 0.5 * (pivots[r] * root) * root)
        scaled.append(rows[r] * root)
    return jnp.concatenate(scaled, axis=0)


def factor_kernel(basis, gram, high_in, low_in, core, subspace, high, low, sem):
    copies = []
    for f in range(high.shape[0]):
        for s, (src, dst) in enumerate(((high_in, high), (low_in, low))):
            copy = pltpu.make_async_copy(src.at[f], dst.at[f], sem.at[f, s])
            copy.start()
            copies.append(copy)
    k, z = basis.shape
    subspace[...] = basis[...]
    row = lax.broadcasted_iota(jnp.int32, (k, 2 * k), 0)
    lane = lax.broadcasted_iota(jnp.int32, (k, 2 * k), 1)
    identity = jnp.where(lane == row + k, 1.0, 0.0).astype(F32)

    def iterate(_, carry):
        product = jnp.concatenate(
            [
                lax.dot_general(subspace[...], gram[h], NN, precision=HIGHEST, preferred_element_type=F32)
                for h in range(2)
            ],
            axis=1,
        )
        zeros = jnp.zeros_like(product)
        square = lax.dot_general(
            product, jnp.concatenate([product, zeros], axis=0), NT, precision=HIGHEST, preferred_element_type=F32
        )
        inverse = inverse_cholesky(square + identity)
        subspace[...] = lax.dot_general(
            inverse, jnp.concatenate([zeros, product], axis=0), NN, precision=HIGHEST, preferred_element_type=F32
        )
        return carry

    lax.fori_loop(0, ITERS, iterate, 0)
    s_high, s_low = split(subspace[...])
    both = jnp.concatenate([s_high, s_low], axis=0)
    for f in range(high.shape[0]):
        copies[2 * f].wait()
        copies[2 * f + 1].wait()
        first = dot(both, high[f], NN)
        result = first[:k] + first[k:] + dot(s_high, low[f], NN)
        for x in range(core.shape[1]):
            core[f, x] = result[:, 128 * x : 128 * x + 128]


def factor(basis, gram, high, low, cells):
    f, z, columns = high.shape
    k = basis.shape[0]
    vmem = pl.BlockSpec(memory_space=pltpu.VMEM)
    return pl.pallas_call(
        factor_kernel,
        name="factor",
        out_shape=jax.ShapeDtypeStruct((f, cells, k, columns // cells), F32),
        in_specs=[vmem, vmem, pl.BlockSpec(memory_space=pl.ANY), pl.BlockSpec(memory_space=pl.ANY)],
        out_specs=vmem,
        scratch_shapes=[
            pltpu.VMEM((k, z), F32),
            pltpu.VMEM((f, z, columns), BF16),
            pltpu.VMEM((f, z, columns), BF16),
            pltpu.SemaphoreType.DMA((f, 2)),
        ],
        compiler_params=pltpu.CompilerParams(vmem_limit_bytes=48 * 2**20),
    )(basis, gram, high, low)


def local(velocity, initial_basis):
    n_ta, n_af = lax.axis_size("ta"), lax.axis_size("af")
    gram, high, low = regroup(velocity, n_ta, n_af)
    return factor(initial_basis.T, gram, high, low, velocity.shape[2] // n_af)


def solution(mesh):
    placed = (P(None, ("ta", "af"), None, None), P())
    return jax.shard_map(
        local, mesh=mesh, in_specs=placed, out_specs=P("ta", "af", None, None), check_vma=False
    )
```

time: 288 us -> 110 us (0.38)
  waiting for transfers between devices: 144 us -> 0 us
  Pallas kernels: 0 us -> 110 us
  blocking collectives: 64 us -> 0 us
  other arithmetic: 36.4 us -> 0 us
  matrix products: 21.3 us -> 0 us
  between operations: 13.5 us -> 0.2 us
  local copies, waits for them, and re-layouts: 8.09 us -> 0.01 us
    psum x1 -> x0, waiting for transfers between devices: 144 us -> none  [local(): gram_matrix = lax.psum(gram_local, ('ta', 'af'))]
    pallas_call x0 -> x2, Pallas kernels: none -> 110 us  [the longest x1 98.4 us: regroup(): pl.pallas_call(functools.partial(regroup_kernel, n_ta, n_af), name='regro...]
    all_to_all x1 -> x0, blocking collectives: 64 us -> none  [local(): lax.all_to_all(blocked, ('ta', 'af'), split_axis=0, concat_axis=2, tiled=...]
    another operation x15 -> x0, other arithmetic: 36.3 us -> none  [the longest x9 19.7 us: orthonormal(): jnp.linalg.cholesky(jnp.dot(product.T, product, precision=lax.Precision.H...]
    dot_general x8 -> x0, matrix products: 20.3 us -> none  [the longest x1 7.93 us: local(): jnp.einsum('fzxy,fwxy->zw', fibres, fibres, precision=lax.Precision.HIGHE...]
    reshape x1 -> x0, local copies, waits for them, and re-layouts: 4.96 us -> none  [local(): velocity.reshape(groups_ta, frames // groups_ta, slab_planes, groups_af,...]
  transfers between devices with their start and end apart: 1 -> 0, of which waited for: 1 -> 0; matrix products, arithmetic and copies ran while one was open for 0% -> 0% of each run, Pallas kernels for 0% -> 0%
where the time goes in v1:
time: 110 us
  Pallas kernels  110 us (100%)
    pallas_call x1, Pallas kernels, regroup(): pl.pallas_call(functools.partial(regroup_kernel, n_ta, n_af), name='regro...  98.4 us
    pallas_call x1, Pallas kernels, factor(): pl.pallas_call(factor_kernel, name='factor', out_shape=jax.ShapeDtypeStru...  11.5 us

profile of v1, /device:TPU:1, one launch (start us, length us, event | category | flops | bytes accessed | tf_op | source)
XLA Modules:
  0.0 110.1 jit_solution(18069527547356421733)
XLA Ops:
  0.0 0.0 copy-start
  0.0 98.4 %regroup.1 = (f32[2,512,256]{2,1,0:T(8,128)S(1)}, bf16[2,512,1024]{2,1,0:T(8,128)(2,1)S(1)}, bf16[2,512,1024]{2,1,0:T(8,128)(2,1)S(1)}) custom-call(f32[16,4,128,128]{3,2,1,0:T(8,128)} %velocity.1), custom_call_target="tpu_custom_call" | custom-call | tf_op jit(solution)/shard_map/regroup/pallas_call | solution.py:134
  98.4 0.0 copy-done
  98.4 11.5 %factor.1 = f32[2,8,64,128]{3,2,1,0:T(8,128)} custom-call(f32[64,512]{1,0:T(8,128)S(1)} %bitcast.1, f32[2,512,256]{2,1,0:T(8,128)S(1)} %get-tuple-element.8.gram, bf16[2,512,1024]{2,1,0:T(8,128)(2,1)S(1)} %get-tuple-element.9.high_in, bf16[2,512,1024]{2,1,0:T(8,128)(2,1)S(1)} %get-tuple-element.10.low_in), custom_call_target="tpu_custom_call" | custom-call | tf_op jit(solution)/shard_map/factor/pallas_call | solution.py:251
Async XLA Ops:
  0.0 98.4 %copy-start = (f32[512,64]{0,1:T(8,128)S(1)}, f32[512,64]{0,1:T(8,128)}, u32[]{:S(2)}) copy-start(f32[512,64]{0,1:T(8,128)} %param.3) | copy-start | bytes 393220

commit v2 on v1

v2 whole, which is shorter than its diff:
```python
import functools
import itertools
import random

import jax
import jax.numpy as jnp
from jax import lax
from jax.experimental import pallas as pl
from jax.experimental.pallas import tpu as pltpu
from jax.sharding import PartitionSpec as P

ITERS = 3
MESH = pl.DeviceIdType.MESH
HIGHEST = lax.Precision.HIGHEST
F32, BF16 = jnp.float32, jnp.bfloat16
NN = (((1,), (0,)), ((), ()))
NT = (((1,), (1,)), ((), ()))


def offsets(n_ta, n_af):
    order = [o for o in itertools.product(range(n_ta), range(n_af)) if o != (0, 0)]
    random.Random(0).shuffle(order)
    return order


def split(value):
    high = value.astype(BF16)
    return high, (value - high.astype(F32)).astype(BF16)


def dot(a, b, dims):
    return lax.dot_general(a, b, dims, preferred_element_type=F32)


def exact(a, b, dims):
    return lax.dot_general(a, b, dims, precision=HIGHEST, preferred_element_type=F32)


def wait_bytes(ref, sem):
    pltpu.make_async_copy(ref, ref, sem).wait()


HALVES = (((0, 0), (0, 1), (1, 1), (0, 2), (0, 3)), ((1, 2), (1, 3), (2, 2), (2, 3), (3, 3)))
CHUNKS = ((0, 0, 8), (1, 0, 4), (1, 4, 4))


def regroup_kernel(
    n_ta, n_af, velocity, gathered, high, low, fibres, partial, other, packed, pieces,
    send_sem, recv_sem, own_sem, pair_send, pair_recv, rs_send, rs_recv, ag_send, ag_recv, last_send, last_recv,
):
    n = n_ta * n_af
    ta, af = lax.axis_index("ta"), lax.axis_index("af")
    me = ta * n_af + af
    core, chip = lax.rem(ta, 2), (ta // 2) * n_af + af
    partner = (ta + 1 - 2 * core, af)
    frames, planes, cells = fibres.shape[0], velocity.shape[1], fibres.shape[2]
    order = offsets(n_ta, n_af)
    same_core = [(i, j) for i, j in order if i % 2 == 0]
    tas = [lax.rem(ta + i, n_ta) for i in range(n_ta)]
    afs = [lax.rem(af + j, n_af) for j in range(n_af)]

    def source(t, a, f, x, w):
        return velocity.at[frames * t + f, :, pl.ds(pl.multiple_of(cells * a + x, w), w), :]

    def arrived(f, x, w):
        return fibres.at[f, pl.ds(planes * me, planes), pl.ds(x, w)]

    own = []
    for c, (f, x, w) in enumerate(CHUNKS):
        copy = pltpu.make_async_copy(source(ta, af, f, x, w), arrived(f, x, w), own_sem.at[c])
        copy.start()
        own.append(copy)

    barrier = pltpu.get_barrier_semaphore()
    for i, j in order:
        pl.semaphore_signal(barrier, inc=1, device_id=(tas[i], afs[j]), device_id_type=MESH)
    pl.semaphore_wait(barrier, n - 1)

    def send(src, dst, sems, device):
        copy = pltpu.make_async_remote_copy(
            src_ref=src, dst_ref=dst, send_sem=sems[0], recv_sem=sems[1], device_id=device, device_id_type=MESH
        )
        copy.start()
        return copy

    for c, (f, x, w) in enumerate(CHUNKS):
        for i, j in order:
            send(source(tas[i], afs[j], f, x, w), arrived(f, x, w), (send_sem.at[c], recv_sem.at[c]), (tas[i], afs[j]))

    def others(f, x, w):
        return fibres.at[f, pl.ds(0, planes * (n - 1)), pl.ds(x, w)]

    for c, (f, x, w) in enumerate(CHUNKS):
        own[c].wait()
        wait_bytes(others(f, x, w), recv_sem.at[c])
        for cell in range(x, x + w):
            h, l = split(fibres[f, :, cell, :])
            high[f, :, 128 * cell : 128 * cell + 128] = h
            low[f, :, 128 * cell : 128 * cell + 128] = l
        lanes = slice(128 * x, 128 * x + 128 * w)
        for top, left in ((0, 0), (0, 2), (2, 2)):
            rows, columns = slice(128 * top, 128 * top + 256), slice(128 * left, 128 * left + 256)
            term = (
                dot(high[f, rows, lanes], high[f, columns, lanes], NT)
                + dot(low[f, rows, lanes], high[f, columns, lanes], NT)
                + dot(high[f, rows, lanes], low[f, columns, lanes], NT)
            )
            for s, half in enumerate(HALVES):
                for k, (row, column) in enumerate(half):
                    if row - top in (0, 1) and column - left in (0, 1):
                        u, v = 128 * (row - top), 128 * (column - left)
                        block = term[u : u + 128, v : v + 128]
                        partial[s, k] = block if c == 0 else partial[s, k] + block
    for c, (f, x, w) in enumerate(CHUNKS):
        wait_bytes(others(f, x, w), send_sem.at[c])

    exchange = send(partial.at[1 - core], other, (pair_send, pair_recv), partner)
    exchange.wait_recv()
    for k in range(len(HALVES[0])):
        block = partial[core, k] + other[k]
        packed[:, 2 * k, :] = block[:64]
        packed[:, 2 * k + 1, :] = block[64:]
    for i, j in same_core:
        send(packed.at[(tas[i] // 2) * n_af + afs[j]], pieces.at[chip], (rs_send, rs_recv), (tas[i], afs[j]))
    pieces[chip] = packed[chip]
    rest = pieces.at[pl.ds(0, n // 2 - 1)]
    wait_bytes(rest, rs_recv)
    gathered[core, chip] = jnp.sum(pieces[...], axis=0)
    for i, j in same_core:
        send(gathered.at[core, chip], gathered.at[core, chip], (ag_send, ag_recv), (tas[i], afs[j]))
    exchange.wait_send()
    wait_bytes(rest, rs_send)
    wait_bytes(rest, ag_recv)
    send(gathered.at[core], gathered.at[core], (last_send, last_recv), partner).wait()
    wait_bytes(rest, ag_send)


def regroup(velocity, n_ta, n_af):
    frames, planes, cells, cells_y = velocity.shape
    n = n_ta * n_af
    f, z, x = frames // n_ta, planes * n, cells // n_af
    blocks = len(HALVES[0])
    vmem = pl.BlockSpec(memory_space=pltpu.VMEM)
    dma = pltpu.SemaphoreType.DMA
    return pl.pallas_call(
        functools.partial(regroup_kernel, n_ta, n_af),
        name="regroup",
        out_shape=(
            jax.ShapeDtypeStruct((2, n // 2, 2 * blocks, 128), F32),
            jax.ShapeDtypeStruct((f, z, x * cells_y), BF16),
            jax.ShapeDtypeStruct((f, z, x * cells_y), BF16),
        ),
        in_specs=[pl.BlockSpec(memory_space=pl.ANY)],
        out_specs=(vmem, vmem, vmem),
        scratch_shapes=[
            pltpu.VMEM((f, z, x, cells_y), F32),
            pltpu.VMEM((2, blocks, 128, 128), F32),
            pltpu.VMEM((blocks, 128, 128), F32),
            pltpu.VMEM((n // 2, 2 * blocks, 128), F32),
            pltpu.VMEM((n // 2, 2 * blocks, 128), F32),
            dma((len(CHUNKS),)), dma((len(CHUNKS),)), dma((len(CHUNKS),)),
            dma, dma, dma, dma, dma, dma, dma, dma,
        ],
        compiler_params=pltpu.CompilerParams(
            collective_id=0, has_side_effects=True, vmem_limit_bytes=48 * 2**20
        ),
    )(velocity)


def inverse_cholesky(matrix):
    k, width = matrix.shape
    groups = k // 8
    rows = [matrix[8 * r : 8 * r + 8, :] for r in range(groups)]
    sublane = lax.broadcasted_iota(jnp.int32, (8, width), 0)
    spread = lambda v, c: jnp.broadcast_to(v[c : c + 1, :], (8, width))
    pivots = []
    for g in range(groups):
        columns = [
            [jnp.broadcast_to(rows[r][:, 8 * g + c : 8 * g + c + 1], (8, width)) for r in range(g, groups)]
            for c in range(8)
        ]
        diagonal = None
        for c in range(8):
            pivot = spread(columns[c][0], c)
            diagonal = pivot if c == 0 else jnp.where(sublane == c, pivot, diagonal)
            inverse = pl.reciprocal(pivot, approx=False)
            pivot_row = spread(rows[g], c)
            pivot_columns = {d: spread(columns[d][0], c) for d in range(c + 1, 8)}
            for r in range(g, groups):
                factor = columns[c][r - g] * inverse
                if r == g:
                    factor = jnp.where(sublane > c, factor, 0.0)
                rows[r] = rows[r] - factor * pivot_row
                for d in range(c + 1, 8):
                    columns[d][r - g] = columns[d][r - g] - factor * pivot_columns[d]
        pivots.append(diagonal)
    scaled = []
    for r in range(groups):
        root = lax.rsqrt(pivots[r])
        root = root * (1.5 - 0.5 * (pivots[r] * root) * root)
        scaled.append(rows[r] * root)
    return jnp.concatenate(scaled, axis=0)


def factor_kernel(basis, gathered, high, low, core, subspace, gram):
    for half, blocks in enumerate(HALVES):
        for k, (row, column) in enumerate(blocks):
            block = jnp.concatenate([gathered[half, :, 2 * k, :], gathered[half, :, 2 * k + 1, :]], axis=0)
            rows, columns = slice(128 * row, 128 * row + 128), slice(128 * column, 128 * column + 128)
            gram[rows, columns] = block
            if row != column:
                gram[columns, rows] = block.T
    k, z = basis.shape
    subspace[...] = basis[...]
    row = lax.broadcasted_iota(jnp.int32, (k, 2 * k), 0)
    lane = lax.broadcasted_iota(jnp.int32, (k, 2 * k), 1)
    identity = jnp.where(lane == row + k, 1.0, 0.0).astype(F32)

    def iterate(_, carry):
        product = exact(subspace[...], gram[...], NN)
        zeros = jnp.zeros_like(product)
        square = exact(product, jnp.concatenate([product, zeros], axis=0), NT)
        inverse = inverse_cholesky(square + identity)
        subspace[...] = exact(inverse, jnp.concatenate([zeros, product], axis=0), NN)
        return carry

    lax.fori_loop(0, ITERS, iterate, 0)
    s_high, s_low = split(subspace[...])
    both = jnp.concatenate([s_high, s_low], axis=0)
    for f in range(high.shape[0]):
        first = dot(both, high[f], NN)
        result = first[:k] + first[k:] + dot(s_high, low[f], NN)
        for x in range(core.shape[1]):
            core[f, x] = result[:, 128 * x : 128 * x + 128]


def factor(basis, gathered, high, low, cells):
    f, z, columns = high.shape
    k = basis.shape[0]
    vmem = pl.BlockSpec(memory_space=pltpu.VMEM)
    return pl.pallas_call(
        factor_kernel,
        name="factor",
        out_shape=jax.ShapeDtypeStruct((f, cells, k, columns // cells), F32),
        in_specs=[vmem] * 4,
        out_specs=vmem,
        scratch_shapes=[pltpu.VMEM((k, z), F32), pltpu.VMEM((z, z), F32)],
        compiler_params=pltpu.CompilerParams(vmem_limit_bytes=24 * 2**20),
    )(basis, gathered, high, low)


def local(velocity, initial_basis):
    n_ta, n_af = lax.axis_size("ta"), lax.axis_size("af")
    gram, high, low = regroup(velocity, n_ta, n_af)
    return factor(initial_basis.T, gram, high, low, velocity.shape[2] // n_af)


def solution(mesh):
    placed = (P(None, ("ta", "af"), None, None), P())
    return jax.shard_map(
        local, mesh=mesh, in_specs=placed, out_specs=P("ta", "af", None, None), check_vma=False
    )
```

time: 110 us -> 94.1 us (0.86)
  Pallas kernels: 110 us -> 93.9 us
    pallas_call x1, Pallas kernels: 98.4 us -> 82.8 us  [regroup(): pl.pallas_call(functools.partial(regroup_kernel, n_ta, n_af), name='regro...]
where the time goes in v2:
time: 94.1 us; the launch traced here: 94 us
  Pallas kernels  93.9 us (100%)
    pallas_call x1, Pallas kernels, regroup(): pl.pallas_call(functools.partial(regroup_kernel, n_ta, n_af), name='regro...  82.8 us
    pallas_call x1, Pallas kernels, factor(): pl.pallas_call(factor_kernel, name='factor', out_shape=jax.ShapeDtypeStru...  11.2 us

profile of v2, /device:TPU:1, one launch (start us, length us, event | category | flops | bytes accessed | tf_op | source)
XLA Modules:
  0.0 94.0 jit_solution(9545642787496665071)
XLA Ops:
  0.0 0.0 copy-start
  0.0 82.8 %regroup.1 = (f32[2,64,10,128]{3,2,1,0:T(8,128)S(1)}, bf16[2,512,1024]{2,1,0:T(8,128)(2,1)S(1)}, bf16[2,512,1024]{2,1,0:T(8,128)(2,1)S(1)}) custom-call(f32[16,4,128,128]{3,2,1,0:T(8,128)} %velocity.1), custom_call_target="tpu_custom_call" | custom-call | tf_op jit(solution)/shard_map/regroup/pallas_call | solution.py:145
  82.8 0.0 copy-done
  82.8 11.2 %factor.1 = f32[2,8,64,128]{3,2,1,0:T(8,128)} custom-call(f32[64,512]{1,0:T(8,128)S(1)} %bitcast.1, f32[2,64,10,128]{3,2,1,0:T(8,128)S(1)} %get-tuple-element.8.gathered, bf16[2,512,1024]{2,1,0:T(8,128)(2,1)S(1)} %get-tuple-element.9.high, bf16[2,512,1024]{2,1,0:T(8,128)(2,1)S(1)} %get-tuple-element.10.low), custom_call_target="tpu_custom_call" | custom-call | tf_op jit(solution)/shard_map/factor/pallas_call | solution.py:241
Async XLA Ops:
  0.0 82.8 %copy-start = (f32[512,64]{0,1:T(8,128)S(1)}, f32[512,64]{0,1:T(8,128)}, u32[]{:S(2)}) copy-start(f32[512,64]{0,1:T(8,128)} %param.3) | copy-start | bytes 393220

commit v3 on v2

--- a/solution.py
+++ b/solution.py
@@ -1,5 +1,6 @@
 import functools
 import itertools
+import math
 import random
 
 import jax
@@ -17,10 +18,11 @@
 NT = (((1,), (1,)), ((), ()))
 
 
-def offsets(n_ta, n_af):
-    order = [o for o in itertools.product(range(n_ta), range(n_af)) if o != (0, 0)]
-    random.Random(0).shuffle(order)
-    return order
+def offsets(n_z, n_x, n_y):
+    order = [o for o in itertools.product(range(n_z), range(2), range(n_x), range(n_y)) if any(o)]
+    random.Random(5).shuffle(order)
+    hops = lambda o: sum(min(d, n - d) for d, n in ((o[0], n_z), (o[2], n_x), (o[3], n_y)))
+    return sorted(order, key=lambda o: -hops(o))
 
 
 def split(value):
@@ -41,7 +43,7 @@
 
 
 HALVES = (((0, 0), (0, 1), (1, 1), (0, 2), (0, 3)), ((1, 2), (1, 3), (2, 2), (2, 3), (3, 3)))
-CHUNKS = ((0, 0, 8), (1, 0, 4), (1, 4, 4))
+CHUNKS = ((0, 0, 8), (1, 0, 6), (1, 6, 2))
 
 
 def regroup_kernel(
@@ -54,13 +56,18 @@
     core, chip = lax.rem(ta, 2), (ta // 2) * n_af + af
     partner = (ta + 1 - 2 * core, af)
     frames, planes, cells = fibres.shape[0], velocity.shape[1], fibres.shape[2]
-    order = offsets(n_ta, n_af)
-    same_core = [(i, j) for i, j in order if i % 2 == 0]
-    tas = [lax.rem(ta + i, n_ta) for i in range(n_ta)]
-    afs = [lax.rem(af + j, n_af) for j in range(n_af)]
+    n_z, side = n_ta // 2, math.isqrt(n_af)
+    z, x_, y_ = ta // 2, af // side, lax.rem(af, side)
+    zs = [lax.rem(z + d, n_z) for d in range(n_z)]
+    tas = [[2 * zs[d] + core, 2 * zs[d] + 1 - core] for d in range(n_z)]
+    xs = [side * lax.rem(x_ + d, side) for d in range(side)]
+    ys = [lax.rem(y_ + d, side) for d in range(side)]
+    afs = [[xs[i] + ys[j] for j in range(side)] for i in range(side)]
+    order = [(tas[d][c], afs[i][j]) for d, c, i, j in offsets(n_z, side, side)]
+    same_core = [(tas[d][0], afs[i][j]) for d, c, i, j in offsets(n_z, side, side) if c == 0]
 
     def source(t, a, f, x, w):
-        return velocity.at[frames * t + f, :, pl.ds(pl.multiple_of(cells * a + x, w), w), :]
+        return velocity.at[frames * t + f, :, pl.ds(pl.multiple_of(cells * a + x, 2), w), :]
 
     def arrived(f, x, w):
         return fibres.at[f, pl.ds(planes * me, planes), pl.ds(x, w)]
@@ -72,8 +79,8 @@
         own.append(copy)
 
     barrier = pltpu.get_barrier_semaphore()
-    for i, j in order:
-        pl.semaphore_signal(barrier, inc=1, device_id=(tas[i], afs[j]), device_id_type=MESH)
+    for device in order:
+        pl.semaphore_signal(barrier, inc=1, device_id=device, device_id_type=MESH)
     pl.semaphore_wait(barrier, n - 1)
 
     def send(src, dst, sems, device):
@@ -84,8 +91,8 @@
         return copy
 
     for c, (f, x, w) in enumerate(CHUNKS):
-        for i, j in order:
-            send(source(tas[i], afs[j], f, x, w), arrived(f, x, w), (send_sem.at[c], recv_sem.at[c]), (tas[i], afs[j]))
+        for t, a in order:
+            send(source(t, a, f, x, w), arrived(f, x, w), (send_sem.at[c], recv_sem.at[c]), (t, a))
 
     def others(f, x, w):
         return fibres.at[f, pl.ds(0, planes * (n - 1)), pl.ds(x, w)]
@@ -120,14 +127,14 @@
         block = partial[core, k] + other[k]
         packed[:, 2 * k, :] = block[:64]
         packed[:, 2 * k + 1, :] = block[64:]
-    for i, j in same_core:
-        send(packed.at[(tas[i] // 2) * n_af + afs[j]], pieces.at[chip], (rs_send, rs_recv), (tas[i], afs[j]))
+    for t, a in same_core:
+        send(packed.at[(t // 2) * n_af + a], pieces.at[chip], (rs_send, rs_recv), (t, a))
     pieces[chip] = packed[chip]
     rest = pieces.at[pl.ds(0, n // 2 - 1)]
     wait_bytes(rest, rs_recv)
     gathered[core, chip] = jnp.sum(pieces[...], axis=0)
-    for i, j in same_core:
-        send(gathered.at[core, chip], gathered.at[core, chip], (ag_send, ag_recv), (tas[i], afs[j]))
+    for device in same_core:
+        send(gathered.at[core, chip], gathered.at[core, chip], (ag_send, ag_recv), device)
     exchange.wait_send()
     wait_bytes(rest, rs_send)
     wait_bytes(rest, ag_recv)
@@ -216,15 +223,15 @@
     lane = lax.broadcasted_iota(jnp.int32, (k, 2 * k), 1)
     identity = jnp.where(lane == row + k, 1.0, 0.0).astype(F32)
 
-    def iterate(_, carry):
+    def iterate():
         product = exact(subspace[...], gram[...], NN)
         zeros = jnp.zeros_like(product)
         square = exact(product, jnp.concatenate([product, zeros], axis=0), NT)
         inverse = inverse_cholesky(square + identity)
         subspace[...] = exact(inverse, jnp.concatenate([zeros, product], axis=0), NN)
-        return carry
-
-    lax.fori_loop(0, ITERS, iterate, 0)
+
+    for _ in range(ITERS):
+        iterate()
     s_high, s_low = split(subspace[...])
     both = jnp.concatenate([s_high, s_low], axis=0)
     for f in range(high.shape[0]):

time: 94.1 us -> 92.2 us (0.980)
  Pallas kernels: 93.9 us -> 92.1 us
    pallas_call x1, Pallas kernels: 82.8 us -> 81.7 us  [regroup(): pl.pallas_call(functools.partial(regroup_kernel, n_ta, n_af), name='regro...]
where the time goes in v3:
time: 92.2 us; the launch traced here: 92.1 us
  Pallas kernels  92.1 us (100%)
    pallas_call x1, Pallas kernels, regroup(): pl.pallas_call(functools.partial(regroup_kernel, n_ta, n_af), name='regro...  81.7 us
    pallas_call x1, Pallas kernels, factor(): pl.pallas_call(factor_kernel, name='factor', out_shape=jax.ShapeDtypeStru...  10.4 us

profile of v3, /device:TPU:1, one launch (start us, length us, event | category | flops | bytes accessed | tf_op | source)
XLA Modules:
  0.0 92.1 jit_solution(6534881237378633595)
XLA Ops:
  0.0 0.0 copy-start
  0.0 81.7 %regroup.1 = (f32[2,64,10,128]{3,2,1,0:T(8,128)S(1)}, bf16[2,512,1024]{2,1,0:T(8,128)(2,1)S(1)}, bf16[2,512,1024]{2,1,0:T(8,128)(2,1)S(1)}) custom-call(f32[16,4,128,128]{3,2,1,0:T(8,128)} %velocity.1), custom_call_target="tpu_custom_call" | custom-call | tf_op jit(solution)/shard_map/regroup/pallas_call | solution.py:152
  81.7 0.0 copy-done
  81.7 10.4 %factor.1 = f32[2,8,64,128]{3,2,1,0:T(8,128)} custom-call(f32[64,512]{1,0:T(8,128)S(1)} %bitcast.1, f32[2,64,10,128]{3,2,1,0:T(8,128)S(1)} %get-tuple-element.8.gathered, bf16[2,512,1024]{2,1,0:T(8,128)(2,1)S(1)} %get-tuple-element.9.high, bf16[2,512,1024]{2,1,0:T(8,128)(2,1)S(1)} %get-tuple-element.10.low), custom_call_target="tpu_custom_call" | custom-call | tf_op jit(solution)/shard_map/factor/pallas_call | solution.py:248
Async XLA Ops:
  0.0 81.7 %copy-start = (f32[512,64]{0,1:T(8,128)S(1)}, f32[512,64]{0,1:T(8,128)}, u32[]{:S(2)}) copy-start(f32[512,64]{0,1:T(8,128)} %param.3) | copy-start | bytes 393220

commit v4 on v3

--- a/solution.py
+++ b/solution.py
@@ -43,7 +43,7 @@
 
 
 HALVES = (((0, 0), (0, 1), (1, 1), (0, 2), (0, 3)), ((1, 2), (1, 3), (2, 2), (2, 3), (3, 3)))
-CHUNKS = ((0, 0, 8), (1, 0, 6), (1, 6, 2))
+CHUNKS = ((0, 0, 8), (1, 0, 4), (1, 4, 4))
 
 
 def regroup_kernel(
@@ -180,26 +180,31 @@
     rows = [matrix[8 * r : 8 * r + 8, :] for r in range(groups)]
     sublane = lax.broadcasted_iota(jnp.int32, (8, width), 0)
     spread = lambda v, c: jnp.broadcast_to(v[c : c + 1, :], (8, width))
+    lane = lambda v, c: jnp.take_along_axis(v, jnp.full((8, width), c, jnp.int32), axis=1)
     pivots = []
+    ahead = {}
     for g in range(groups):
-        columns = [
-            [jnp.broadcast_to(rows[r][:, 8 * g + c : 8 * g + c + 1], (8, width)) for r in range(g, groups)]
-            for c in range(8)
-        ]
+        columns = [{r: ahead[d, r] if (d, r) in ahead else lane(rows[r], 8 * g + d) for r in range(g, groups)} for d in range(8)]
+        late = range(g + 1, min(g + 1 + 1, groups))
+        ahead = {(d, r): lane(rows[r], 8 * g + 8 + d) for r in late for d in range(8)}
         diagonal = None
         for c in range(8):
-            pivot = spread(columns[c][0], c)
+            pivot = spread(columns[c][g], c)
             diagonal = pivot if c == 0 else jnp.where(sublane == c, pivot, diagonal)
-            inverse = pl.reciprocal(pivot, approx=False)
+            inverse = 1.0 / pivot
             pivot_row = spread(rows[g], c)
-            pivot_columns = {d: spread(columns[d][0], c) for d in range(c + 1, 8)}
+            inside = {d: spread(columns[d][g], c) for d in range(c + 1, 8)}
+            outside = {d: spread(columns[c][g + 1], d) for d in range(8)} if g + 1 < groups else {}
             for r in range(g, groups):
-                factor = columns[c][r - g] * inverse
+                factor = columns[c][r] * inverse
                 if r == g:
                     factor = jnp.where(sublane > c, factor, 0.0)
+                for d in range(c + 1, 8):
+                    columns[d][r] = columns[d][r] - factor * inside[d]
+                if r in late:
+                    for d in range(8):
+                        ahead[d, r] = ahead[d, r] - factor * outside[d]
                 rows[r] = rows[r] - factor * pivot_row
-                for d in range(c + 1, 8):
-                    columns[d][r - g] = columns[d][r - g] - factor * pivot_columns[d]
         pivots.append(diagonal)
     scaled = []
     for r in range(groups):
@@ -209,7 +214,7 @@
     return jnp.concatenate(scaled, axis=0)
 
 
-def factor_kernel(basis, gathered, high, low, core, subspace, gram):
+def factor_kernel(basis, gathered, high, low, core, subspace, gram, g1, g2, g3):
     for half, blocks in enumerate(HALVES):
         for k, (row, column) in enumerate(blocks):
             block = jnp.concatenate([gathered[half, :, 2 * k, :], gathered[half, :, 2 * k + 1, :]], axis=0)
@@ -219,12 +224,20 @@
                 gram[columns, rows] = block.T
     k, z = basis.shape
     subspace[...] = basis[...]
+    h, l = split(gram[...])
+    g1[...] = h
+    g2[...] = l
+    g3[...] = (gram[...] - h.astype(F32) - l.astype(F32)).astype(BF16)
     row = lax.broadcasted_iota(jnp.int32, (k, 2 * k), 0)
     lane = lax.broadcasted_iota(jnp.int32, (k, 2 * k), 1)
     identity = jnp.where(lane == row + k, 1.0, 0.0).astype(F32)
 
     def iterate():
-        product = exact(subspace[...], gram[...], NN)
+        s1, s2 = split(subspace[...])
+        s3 = (subspace[...] - s1.astype(F32) - s2.astype(F32)).astype(BF16)
+        t1 = dot(jnp.concatenate([s1, s2, s3], axis=0), g1[...], NN)
+        t2 = dot(jnp.concatenate([s1, s2], axis=0), g2[...], NN)
+        product = (t2[k:] + (t1[2 * k:] + dot(s1, g3[...], NN))) + (t1[k:2 * k] + t2[:k]) + t1[:k]
         zeros = jnp.zeros_like(product)
         square = exact(product, jnp.concatenate([product, zeros], axis=0), NT)
         inverse = inverse_cholesky(square + identity)
@@ -251,7 +264,7 @@
         out_shape=jax.ShapeDtypeStruct((f, cells, k, columns // cells), F32),
         in_specs=[vmem] * 4,
         out_specs=vmem,
-        scratch_shapes=[pltpu.VMEM((k, z), F32), pltpu.VMEM((z, z), F32)],
+        scratch_shapes=[pltpu.VMEM((k, z), F32), pltpu.VMEM((z, z), F32)] + [pltpu.VMEM((z, z), BF16)] * 3,
         compiler_params=pltpu.CompilerParams(vmem_limit_bytes=24 * 2**20),
     )(basis, gathered, high, low)
 

time: 92.2 us -> 88.5 us (0.960)
  Pallas kernels: 92.1 us -> 88.4 us
    pallas_call x1, Pallas kernels: 10.4 us -> 7.73 us  [factor(): pl.pallas_call(factor_kernel, name='factor', out_shape=jax.ShapeDtypeStru...]
    pallas_call x1, Pallas kernels: 81.7 us -> 80.6 us  [regroup(): pl.pallas_call(functools.partial(regroup_kernel, n_ta, n_af), name='regro...]
where the time goes in v4:
time: 88.5 us; the launch traced here: 88.4 us
  Pallas kernels  88.4 us (100%)
    pallas_call x1, Pallas kernels, regroup(): pl.pallas_call(functools.partial(regroup_kernel, n_ta, n_af), name='regro...  80.6 us
    pallas_call x1, Pallas kernels, factor(): pl.pallas_call(factor_kernel, name='factor', out_shape=jax.ShapeDtypeStru...  7.73 us

profile of v4, /device:TPU:1, one launch (start us, length us, event | category | flops | bytes accessed | tf_op | source)
XLA Modules:
  0.0 88.4 jit_solution(6123434500334321635)
XLA Ops:
  0.0 0.0 copy-start
  0.0 80.6 %regroup.1 = (f32[2,64,10,128]{3,2,1,0:T(8,128)S(1)}, bf16[2,512,1024]{2,1,0:T(8,128)(2,1)S(1)}, bf16[2,512,1024]{2,1,0:T(8,128)(2,1)S(1)}) custom-call(f32[16,4,128,128]{3,2,1,0:T(8,128)} %velocity.1), custom_call_target="tpu_custom_call" | custom-call | tf_op jit(solution)/shard_map/regroup/pallas_call | solution.py:152
  80.6 0.0 copy-done
  80.7 7.7 %factor.1 = f32[2,8,64,128]{3,2,1,0:T(8,128)} custom-call(f32[64,512]{1,0:T(8,128)S(1)} %bitcast.1, f32[2,64,10,128]{3,2,1,0:T(8,128)S(1)} %get-tuple-element.8.gathered, bf16[2,512,1024]{2,1,0:T(8,128)(2,1)S(1)} %get-tuple-element.9.high, bf16[2,512,1024]{2,1,0:T(8,128)(2,1)S(1)} %get-tuple-element.10.low), custom_call_target="tpu_custom_call" | custom-call | tf_op jit(solution)/shard_map/factor/pallas_call | solution.py:261
Async XLA Ops:
  0.0 80.7 %copy-start = (f32[512,64]{0,1:T(8,128)S(1)}, f32[512,64]{0,1:T(8,128)}, u32[]{:S(2)}) copy-start(f32[512,64]{0,1:T(8,128)} %param.3) | copy-start | bytes 393220

commit v5 on v4

--- a/solution.py
+++ b/solution.py
@@ -43,7 +43,8 @@
 
 
 HALVES = (((0, 0), (0, 1), (1, 1), (0, 2), (0, 3)), ((1, 2), (1, 3), (2, 2), (2, 3), (3, 3)))
-CHUNKS = ((0, 0, 8), (1, 0, 4), (1, 4, 4))
+PAD = 16
+CHUNKS = ((0, 0, 8), (1, 0, 4), (1, 4, 2), (1, 6, 2))
 
 
 def regroup_kernel(
@@ -94,6 +95,8 @@
         for t, a in order:
             send(source(t, a, f, x, w), arrived(f, x, w), (send_sem.at[c], recv_sem.at[c]), (t, a))
 
+    flat = fibres.reshape(frames, planes * n * cells, 128)
+
     def others(f, x, w):
         return fibres.at[f, pl.ds(0, planes * (n - 1)), pl.ds(x, w)]
 
@@ -101,7 +104,7 @@
         own[c].wait()
         wait_bytes(others(f, x, w), recv_sem.at[c])
         for cell in range(x, x + w):
-            h, l = split(fibres[f, :, cell, :])
+            h, l = split(flat[f, pl.ds(cell, planes * n, stride=cells), :])
             high[f, :, 128 * cell : 128 * cell + 128] = h
             low[f, :, 128 * cell : 128 * cell + 128] = l
         lanes = slice(128 * x, 128 * x + 128 * w)
@@ -121,24 +124,28 @@
     for c, (f, x, w) in enumerate(CHUNKS):
         wait_bytes(others(f, x, w), send_sem.at[c])
 
+    used = pl.ds(0, 2 * len(HALVES[0]))
     exchange = send(partial.at[1 - core], other, (pair_send, pair_recv), partner)
     exchange.wait_recv()
+    flat_packed = packed.reshape(n // 2 * PAD, 128)
     for k in range(len(HALVES[0])):
         block = partial[core, k] + other[k]
-        packed[:, 2 * k, :] = block[:64]
-        packed[:, 2 * k + 1, :] = block[64:]
+        for part in range(2):
+            flat_packed[pl.ds(2 * k + part, n // 2, stride=PAD), :] = block[64 * part : 64 * part + 64]
     for t, a in same_core:
-        send(packed.at[(t // 2) * n_af + a], pieces.at[chip], (rs_send, rs_recv), (t, a))
+        send(packed.at[(t // 2) * n_af + a, used], pieces.at[chip, used], (rs_send, rs_recv), (t, a))
     pieces[chip] = packed[chip]
-    rest = pieces.at[pl.ds(0, n // 2 - 1)]
+    rest = pieces.at[pl.ds(0, n // 2 - 1), used]
     wait_bytes(rest, rs_recv)
-    gathered[core, chip] = jnp.sum(pieces[...], axis=0)
+    gathered[core, chip, used] = jnp.sum(pieces[:, used, :], axis=0)
+    mine = gathered.at[core, chip, used]
     for device in same_core:
-        send(gathered.at[core, chip], gathered.at[core, chip], (ag_send, ag_recv), device)
+        send(mine, mine, (ag_send, ag_recv), device)
     exchange.wait_send()
     wait_bytes(rest, rs_send)
     wait_bytes(rest, ag_recv)
-    send(gathered.at[core], gathered.at[core], (last_send, last_recv), partner).wait()
+    half = gathered.at[core, :, used]
+    send(half, half, (last_send, last_recv), partner).wait()
     wait_bytes(rest, ag_send)
 
 
@@ -153,7 +160,7 @@
         functools.partial(regroup_kernel, n_ta, n_af),
         name="regroup",
         out_shape=(
-            jax.ShapeDtypeStruct((2, n // 2, 2 * blocks, 128), F32),
+            jax.ShapeDtypeStruct((2, n // 2, PAD, 128), F32),
             jax.ShapeDtypeStruct((f, z, x * cells_y), BF16),
             jax.ShapeDtypeStruct((f, z, x * cells_y), BF16),
         ),
@@ -163,8 +170,8 @@
             pltpu.VMEM((f, z, x, cells_y), F32),
             pltpu.VMEM((2, blocks, 128, 128), F32),
             pltpu.VMEM((blocks, 128, 128), F32),
-            pltpu.VMEM((n // 2, 2 * blocks, 128), F32),
-            pltpu.VMEM((n // 2, 2 * blocks, 128), F32),
+            pltpu.VMEM((n // 2, PAD, 128), F32),
+            pltpu.VMEM((n // 2, PAD, 128), F32),
             dma((len(CHUNKS),)), dma((len(CHUNKS),)), dma((len(CHUNKS),)),
             dma, dma, dma, dma, dma, dma, dma, dma,
         ],
@@ -215,9 +222,10 @@
 
 
 def factor_kernel(basis, gathered, high, low, core, subspace, gram, g1, g2, g3):
+    flat = gathered.reshape(2, gathered.shape[1] * PAD, 128)
     for half, blocks in enumerate(HALVES):
         for k, (row, column) in enumerate(blocks):
-            block = jnp.concatenate([gathered[half, :, 2 * k, :], gathered[half, :, 2 * k + 1, :]], axis=0)
+            block = jnp.concatenate([flat[half, pl.ds(2 * k + p, 64, stride=PAD), :] for p in range(2)], axis=0)
             rows, columns = slice(128 * row, 128 * row + 128), slice(128 * column, 128 * column + 128)
             gram[rows, columns] = block
             if row != column:

time: 88.5 us -> 84.5 us (0.955)
  Pallas kernels: 88.4 us -> 84.3 us
    pallas_call x1, Pallas kernels: 80.6 us -> 76.7 us  [regroup(): pl.pallas_call(functools.partial(regroup_kernel, n_ta, n_af), name='regro...]
where the time goes in v5:
time: 84.5 us; the launch traced here: 84.4 us
  Pallas kernels  84.3 us (100%)
    pallas_call x1, Pallas kernels, regroup(): pl.pallas_call(functools.partial(regroup_kernel, n_ta, n_af), name='regro...  76.7 us
    pallas_call x1, Pallas kernels, factor(): pl.pallas_call(factor_kernel, name='factor', out_shape=jax.ShapeDtypeStru...  7.62 us

profile of v5, /device:TPU:1, one launch (start us, length us, event | category | flops | bytes accessed | tf_op | source)
XLA Modules:
  0.0 84.4 jit_solution(1554273634548648489)
XLA Ops:
  0.0 0.0 copy-start
  0.0 76.7 %regroup.1 = (f32[2,64,16,128]{3,2,1,0:T(8,128)S(1)}, bf16[2,512,1024]{2,1,0:T(8,128)(2,1)S(1)}, bf16[2,512,1024]{2,1,0:T(8,128)(2,1)S(1)}) custom-call(f32[16,4,128,128]{3,2,1,0:T(8,128)} %velocity.1), custom_call_target="tpu_custom_call" | custom-call | tf_op jit(solution)/shard_map/regroup/pallas_call | solution.py:159
  76.7 0.0 copy-done
  76.8 7.6 %factor.1 = f32[2,8,64,128]{3,2,1,0:T(8,128)} custom-call(f32[64,512]{1,0:T(8,128)S(1)} %bitcast.1, f32[2,64,16,128]{3,2,1,0:T(8,128)S(1)} %get-tuple-element.8.gathered, bf16[2,512,1024]{2,1,0:T(8,128)(2,1)S(1)} %get-tuple-element.9.high, bf16[2,512,1024]{2,1,0:T(8,128)(2,1)S(1)} %get-tuple-element.10.low), custom_call_target="tpu_custom_call" | custom-call | tf_op jit(solution)/shard_map/factor/pallas_call | solution.py:269
Async XLA Ops:
  0.0 76.7 %copy-start = (f32[512,64]{0,1:T(8,128)S(1)}, f32[512,64]{0,1:T(8,128)}, u32[]{:S(2)}) copy-start(f32[512,64]{0,1:T(8,128)} %param.3) | copy-start | bytes 393220

commit v6 on v5

--- a/solution.py
+++ b/solution.py
@@ -21,8 +21,11 @@
 def offsets(n_z, n_x, n_y):
     order = [o for o in itertools.product(range(n_z), range(2), range(n_x), range(n_y)) if any(o)]
     random.Random(5).shuffle(order)
-    hops = lambda o: sum(min(d, n - d) for d, n in ((o[0], n_z), (o[2], n_x), (o[3], n_y)))
-    return sorted(order, key=lambda o: -hops(o))
+    return sorted(order, key=lambda o: -hops(o, n_z, n_x, n_y))
+
+
+def hops(offset, n_z, n_x, n_y):
+    return sum(min(d, n - d) for d, n in ((offset[0], n_z), (offset[2], n_x), (offset[3], n_y)))
 
 
 def split(value):
@@ -65,7 +68,11 @@
     ys = [lax.rem(y_ + d, side) for d in range(side)]
     afs = [[xs[i] + ys[j] for j in range(side)] for i in range(side)]
     order = [(tas[d][c], afs[i][j]) for d, c, i, j in offsets(n_z, side, side)]
-    same_core = [(tas[d][0], afs[i][j]) for d, c, i, j in offsets(n_z, side, side) if c == 0]
+    same_core = [
+        ((tas[d][0], afs[i][j]), int(hops((d, 0, i, j), n_z, side, side) > (n_z + 2 * side) // 4))
+        for d, c, i, j in offsets(n_z, side, side)
+        if c == 0
+    ]
 
     def source(t, a, f, x, w):
         return velocity.at[frames * t + f, :, pl.ds(pl.multiple_of(cells * a + x, 2), w), :]
@@ -132,21 +139,27 @@
         block = partial[core, k] + other[k]
         for part in range(2):
             flat_packed[pl.ds(2 * k + part, n // 2, stride=PAD), :] = block[64 * part : 64 * part + 64]
-    for t, a in same_core:
+    for (t, a), _ in same_core:
         send(packed.at[(t // 2) * n_af + a, used], pieces.at[chip, used], (rs_send, rs_recv), (t, a))
     pieces[chip] = packed[chip]
     rest = pieces.at[pl.ds(0, n // 2 - 1), used]
     wait_bytes(rest, rs_recv)
     gathered[core, chip, used] = jnp.sum(pieces[:, used, :], axis=0)
     mine = gathered.at[core, chip, used]
-    for device in same_core:
-        send(mine, mine, (ag_send, ag_recv), device)
+    for device, far in same_core:
+        send(mine, mine, (ag_send, ag_recv.at[far]), device)
     exchange.wait_send()
     wait_bytes(rest, rs_send)
-    wait_bytes(rest, ag_recv)
-    half = gathered.at[core, :, used]
-    send(half, half, (last_send, last_recv), partner).wait()
+    send(mine, mine, (last_send, last_recv), partner)
+    for far in range(2):
+        group = [device for device, f in same_core if f == far]
+        wait_bytes(pieces.at[pl.ds(0, len(group)), used], ag_recv.at[far])
+        for t, a in group:
+            share = gathered.at[core, (t // 2) * n_af + a, used]
+            send(share, share, (last_send, last_recv), partner)
     wait_bytes(rest, ag_send)
+    wait_bytes(pieces.at[:, used], last_send)
+    wait_bytes(pieces.at[:, used], last_recv)
 
 
 def regroup(velocity, n_ta, n_af):
@@ -173,7 +186,7 @@
             pltpu.VMEM((n // 2, PAD, 128), F32),
             pltpu.VMEM((n // 2, PAD, 128), F32),
             dma((len(CHUNKS),)), dma((len(CHUNKS),)), dma((len(CHUNKS),)),
-            dma, dma, dma, dma, dma, dma, dma, dma,
+            dma, dma, dma, dma, dma, dma((2,)), dma, dma,
         ],
         compiler_params=pltpu.CompilerParams(
             collective_id=0, has_side_effects=True, vmem_limit_bytes=48 * 2**20
@@ -181,7 +194,7 @@
     )(velocity)
 
 
-def inverse_cholesky(matrix):
+def inverse_cholesky(matrix, beside):
     k, width = matrix.shape
     groups = k // 8
     rows = [matrix[8 * r : 8 * r + 8, :] for r in range(groups)]
@@ -213,6 +226,8 @@
                         ahead[d, r] = ahead[d, r] - factor * outside[d]
                 rows[r] = rows[r] - factor * pivot_row
         pivots.append(diagonal)
+        if g in beside:
+            beside[g]()
     scaled = []
     for r in range(groups):
         root = lax.rsqrt(pivots[r])
@@ -240,19 +255,30 @@
     lane = lax.broadcasted_iota(jnp.int32, (k, 2 * k), 1)
     identity = jnp.where(lane == row + k, 1.0, 0.0).astype(F32)
 
-    def iterate():
-        s1, s2 = split(subspace[...])
-        s3 = (subspace[...] - s1.astype(F32) - s2.astype(F32)).astype(BF16)
-        t1 = dot(jnp.concatenate([s1, s2, s3], axis=0), g1[...], NN)
-        t2 = dot(jnp.concatenate([s1, s2], axis=0), g2[...], NN)
-        product = (t2[k:] + (t1[2 * k:] + dot(s1, g3[...], NN))) + (t1[k:2 * k] + t2[:k]) + t1[:k]
+    def times_gram(value, lanes):
+        s1, s2 = split(value)
+        s3 = (value - s1.astype(F32) - s2.astype(F32)).astype(BF16)
+        t1 = dot(jnp.concatenate([s1, s2, s3], axis=0), g1[:, lanes], NN)
+        t2 = dot(jnp.concatenate([s1, s2], axis=0), g2[:, lanes], NN)
+        small = t2[k:] + (t1[2 * k :] + dot(s1, g3[:, lanes], NN))
+        return small + (t1[k : 2 * k] + t2[:k]) + t1[:k]
+
+    product = times_gram(subspace[...], slice(0, z))
+    for step in range(ITERS):
         zeros = jnp.zeros_like(product)
         square = exact(product, jnp.concatenate([product, zeros], axis=0), NT)
-        inverse = inverse_cholesky(square + identity)
-        subspace[...] = exact(inverse, jnp.concatenate([zeros, product], axis=0), NN)
-
-    for _ in range(ITERS):
-        iterate()
+        beside = {}
+        if step < ITERS - 1:
+
+            def piece(i, value=product):
+                lanes = slice(i * z // 1, (i + 1) * z // 1)
+                subspace[:, lanes] = times_gram(value, lanes)
+
+            beside = {g: functools.partial(piece, i) for i, g in enumerate((0,))}
+        inverse = inverse_cholesky(square + identity, beside)
+        target = subspace[...] if step < ITERS - 1 else product
+        product = exact(inverse, jnp.concatenate([zeros, target], axis=0), NN)
+    subspace[...] = product
     s_high, s_low = split(subspace[...])
     both = jnp.concatenate([s_high, s_low], axis=0)
     for f in range(high.shape[0]):

time: 84.5 us -> 83.7 us (level)
  no operation moved by 1% of the time
where the time goes in v6:
time: 83.7 us; the launch traced here: 83.6 us
  Pallas kernels  83.5 us (100%)
    pallas_call x1, Pallas kernels, regroup(): pl.pallas_call(functools.partial(regroup_kernel, n_ta, n_af), name='regro...  76.7 us
    pallas_call x1, Pallas kernels, factor(): pl.pallas_call(factor_kernel, name='factor', out_shape=jax.ShapeDtypeStru...  6.81 us

profile of v6, /device:TPU:1, one launch (start us, length us, event | category | flops | bytes accessed | tf_op | source)
XLA Modules:
  0.0 83.6 jit_solution(238174615499911978)
XLA Ops:
  0.0 0.0 copy-start
  0.0 76.7 %regroup.1 = (f32[2,64,16,128]{3,2,1,0:T(8,128)S(1)}, bf16[2,512,1024]{2,1,0:T(8,128)(2,1)S(1)}, bf16[2,512,1024]{2,1,0:T(8,128)(2,1)S(1)}) custom-call(f32[16,4,128,128]{3,2,1,0:T(8,128)} %velocity.1), custom_call_target="tpu_custom_call" | custom-call | tf_op jit(solution)/shard_map/regroup/pallas_call | solution.py:172
  76.7 0.0 copy-done
  76.8 6.8 %factor.1 = f32[2,8,64,128]{3,2,1,0:T(8,128)} custom-call(f32[64,512]{1,0:T(8,128)S(1)} %bitcast.1, f32[2,64,16,128]{3,2,1,0:T(8,128)S(1)} %get-tuple-element.8.gathered, bf16[2,512,1024]{2,1,0:T(8,128)(2,1)S(1)} %get-tuple-element.9.high, bf16[2,512,1024]{2,1,0:T(8,128)(2,1)S(1)} %get-tuple-element.10.low), custom_call_target="tpu_custom_call" | custom-call | tf_op jit(solution)/shard_map/factor/pallas_call | solution.py:295
Async XLA Ops:
  0.0 76.7 %copy-start = (f32[512,64]{0,1:T(8,128)S(1)}, f32[512,64]{0,1:T(8,128)}, u32[]{:S(2)}) copy-start(f32[512,64]{0,1:T(8,128)} %param.3) | copy-start | bytes 393220

commit v7 on v6

--- a/solution.py
+++ b/solution.py
@@ -203,18 +203,22 @@
     lane = lambda v, c: jnp.take_along_axis(v, jnp.full((8, width), c, jnp.int32), axis=1)
     pivots = []
     ahead = {}
+    pivot = spread(lane(rows[0], 0), 0)
     for g in range(groups):
         columns = [{r: ahead[d, r] if (d, r) in ahead else lane(rows[r], 8 * g + d) for r in range(g, groups)} for d in range(8)]
         late = range(g + 1, min(g + 1 + 1, groups))
         ahead = {(d, r): lane(rows[r], 8 * g + 8 + d) for r in late for d in range(8)}
         diagonal = None
         for c in range(8):
-            pivot = spread(columns[c][g], c)
             diagonal = pivot if c == 0 else jnp.where(sublane == c, pivot, diagonal)
             inverse = 1.0 / pivot
             pivot_row = spread(rows[g], c)
             inside = {d: spread(columns[d][g], c) for d in range(c + 1, 8)}
             outside = {d: spread(columns[c][g + 1], d) for d in range(8)} if g + 1 < groups else {}
+            if c < 7:
+                pivot = spread(columns[c + 1][g], c + 1) - (spread(columns[c][g], c + 1) * inverse) * inside[c + 1]
+            elif g + 1 < groups:
+                pivot = spread(ahead[0, g + 1], 0) - (outside[0] * inverse) * outside[0]
             for r in range(g, groups):
                 factor = columns[c][r] * inverse
                 if r == g:
@@ -236,7 +240,7 @@
     return jnp.concatenate(scaled, axis=0)
 
 
-def factor_kernel(basis, gathered, high, low, core, subspace, gram, g1, g2, g3):
+def factor_kernel(basis, gathered, high, low, core, subspace, gram, g1, g2, g3, staged, sem):
     flat = gathered.reshape(2, gathered.shape[1] * PAD, 128)
     for half, blocks in enumerate(HALVES):
         for k, (row, column) in enumerate(blocks):
@@ -281,11 +285,17 @@
     subspace[...] = product
     s_high, s_low = split(subspace[...])
     both = jnp.concatenate([s_high, s_low], axis=0)
+    copies = []
     for f in range(high.shape[0]):
         first = dot(both, high[f], NN)
         result = first[:k] + first[k:] + dot(s_high, low[f], NN)
-        for x in range(core.shape[1]):
-            core[f, x] = result[:, 128 * x : 128 * x + 128]
+        for x in range(staged.shape[1]):
+            staged[f, x] = result[:, 128 * x : 128 * x + 128]
+        copy = pltpu.make_async_copy(staged.at[f], core.at[f], sem.at[f])
+        copy.start()
+        copies.append(copy)
+    for copy in copies:
+        copy.wait()
 
 
 def factor(basis, gathered, high, low, cells):
@@ -297,8 +307,10 @@
         name="factor",
         out_shape=jax.ShapeDtypeStruct((f, cells, k, columns // cells), F32),
         in_specs=[vmem] * 4,
-        out_specs=vmem,
-        scratch_shapes=[pltpu.VMEM((k, z), F32), pltpu.VMEM((z, z), F32)] + [pltpu.VMEM((z, z), BF16)] * 3,
+        out_specs=pl.BlockSpec(memory_space=pl.ANY),
+        scratch_shapes=[pltpu.VMEM((k, z), F32), pltpu.VMEM((z, z), F32)]
+        + [pltpu.VMEM((z, z), BF16)] * 3
+        + [pltpu.VMEM((f, cells, k, columns // cells), F32), pltpu.SemaphoreType.DMA((f,))],
         compiler_params=pltpu.CompilerParams(vmem_limit_bytes=24 * 2**20),
     )(basis, gathered, high, low)
 

time: 83.7 us -> 83.3 us (level)
  no operation moved by 1% of the time
where the time goes in v7:
time: 83.3 us; the launch traced here: 83.2 us
  Pallas kernels  83.2 us (100%)
    pallas_call x1, Pallas kernels, regroup(): pl.pallas_call(functools.partial(regroup_kernel, n_ta, n_af), name='regro...  76.7 us
    pallas_call x1, Pallas kernels, factor(): pl.pallas_call(factor_kernel, name='factor', out_shape=jax.ShapeDtypeStru...  6.48 us

profile of v7, /device:TPU:1, one launch (start us, length us, event | category | flops | bytes accessed | tf_op | source)
XLA Modules:
  0.0 83.2 jit_solution(3134030568797070327)
XLA Ops:
  0.0 0.0 copy-start
  0.0 76.7 %regroup.1 = (f32[2,64,16,128]{3,2,1,0:T(8,128)S(1)}, bf16[2,512,1024]{2,1,0:T(8,128)(2,1)S(1)}, bf16[2,512,1024]{2,1,0:T(8,128)(2,1)S(1)}) custom-call(f32[16,4,128,128]{3,2,1,0:T(8,128)} %velocity.1), custom_call_target="tpu_custom_call" | custom-call | tf_op jit(solution)/shard_map/regroup/pallas_call | solution.py:172
  76.7 0.0 copy-done
  76.8 6.5 %factor.1 = f32[2,8,64,128]{3,2,1,0:T(8,128)} custom-call(f32[64,512]{1,0:T(8,128)S(1)} %bitcast.1, f32[2,64,16,128]{3,2,1,0:T(8,128)S(1)} %get-tuple-element.8.gathered, bf16[2,512,1024]{2,1,0:T(8,128)(2,1)S(1)} %get-tuple-element.9.high, bf16[2,512,1024]{2,1,0:T(8,128)(2,1)S(1)} %get-tuple-element.10.low), custom_call_target="tpu_custom_call" | custom-call | tf_op jit(solution)/shard_map/factor/pallas_call | solution.py:305
Async XLA Ops:
  0.0 76.7 %copy-start = (f32[512,64]{0,1:T(8,128)S(1)}, f32[512,64]{0,1:T(8,128)}, u32[]{:S(2)}) copy-start(f32[512,64]{0,1:T(8,128)} %param.3) | copy-start | bytes 393220

commit v8 on v7

--- a/solution.py
+++ b/solution.py
@@ -47,7 +47,7 @@
 
 HALVES = (((0, 0), (0, 1), (1, 1), (0, 2), (0, 3)), ((1, 2), (1, 3), (2, 2), (2, 3), (3, 3)))
 PAD = 16
-CHUNKS = ((0, 0, 8), (1, 0, 4), (1, 4, 2), (1, 6, 2))
+CHUNKS = ((0, 0, 8), (1, 0, 4), (1, 4, 4))
 
 
 def regroup_kernel(

time: 83.3 us -> 83.6 us (level)
  no operation moved by 1% of the time
where the time goes in v8:
time: 83.6 us; the launch traced here: 83.5 us
  Pallas kernels  83.4 us (100%)
    pallas_call x1, Pallas kernels, regroup(): pl.pallas_call(functools.partial(regroup_kernel, n_ta, n_af), name='regro...  77 us
    pallas_call x1, Pallas kernels, factor(): pl.pallas_call(factor_kernel, name='factor', out_shape=jax.ShapeDtypeStru...  6.49 us

profile of v8, /device:TPU:1, one launch (start us, length us, event | category | flops | bytes accessed | tf_op | source)
XLA Modules:
  0.0 83.5 jit_solution(7110250302903490849)
XLA Ops:
  0.0 0.0 copy-start
  0.0 77.0 %regroup.1 = (f32[2,64,16,128]{3,2,1,0:T(8,128)S(1)}, bf16[2,512,1024]{2,1,0:T(8,128)(2,1)S(1)}, bf16[2,512,1024]{2,1,0:T(8,128)(2,1)S(1)}) custom-call(f32[16,4,128,128]{3,2,1,0:T(8,128)} %velocity.1), custom_call_target="tpu_custom_call" | custom-call | tf_op jit(solution)/shard_map/regroup/pallas_call | solution.py:172
  77.0 0.0 copy-done
  77.0 6.5 %factor.1 = f32[2,8,64,128]{3,2,1,0:T(8,128)} custom-call(f32[64,512]{1,0:T(8,128)S(1)} %bitcast.1, f32[2,64,16,128]{3,2,1,0:T(8,128)S(1)} %get-tuple-element.8.gathered, bf16[2,512,1024]{2,1,0:T(8,128)(2,1)S(1)} %get-tuple-element.9.high, bf16[2,512,1024]{2,1,0:T(8,128)(2,1)S(1)} %get-tuple-element.10.low), custom_call_target="tpu_custom_call" | custom-call | tf_op jit(solution)/shard_map/factor/pallas_call | solution.py:305
Async XLA Ops:
  0.0 77.0 %copy-start = (f32[512,64]{0,1:T(8,128)S(1)}, f32[512,64]{0,1:T(8,128)}, u32[]{:S(2)}) copy-start(f32[512,64]{0,1:T(8,128)} %param.3) | copy-start | bytes 393220
